TPU v7x, 32 devices: a whole 2x2x4 slice. The times are simulated.
32 devices in a mesh: gx: 4 (over y, core), gy: 4 (over z), gz: 2 (over x).
Axes of the slice: x: 2, y: 2, z: 4, core: 2. Of those that a mesh axis runs over, the one named last changes fastest.
Arguments:
- positions: float32 [4, 16, 2, 3, 128], P('gx', 'gy', 'gz'), may hold values from 0 to 1
- velocities: float32 [4, 16, 2, 3, 128], P('gx', 'gy', 'gz'), may hold values from -6 to 6
- charges: float32 [4, 16, 2, 128], P('gx', 'gy', 'gz'), may hold values from -3 to 3
- atom_types: int32 [4, 16, 2, 128], P('gx', 'gy', 'gz'), may hold values from 0 to 15
- atom_count: int32 [4, 16, 2], P('gx', 'gy', 'gz'), may hold values from 32 to 128
- sigma_type: float32 [16], replicated, may hold values from 0.15 to 0.35
- epsilon_type: float32 [16], replicated, may hold values from 0.3 to 3
- masses: float32 [4, 16, 2, 128], P('gx', 'gy', 'gz'), may hold values from 1 to 4
- pair_list: int32 [4, 4, 2, 2, 56], P('gx', 'gy', 'gz'), may hold values from 0 to 19, as said below
- pair_count: int32 [4, 4, 2], P('gx', 'gy', 'gz'), may hold values from 1 to 56, as said below
- pos_cotangent: float32 [4, 16, 2, 3, 128], P('gx', 'gy', 'gz'), may hold values from -6 to 6
- vel_cotangent: float32 [4, 16, 2, 3, 128], P('gx', 'gy', 'gz'), may hold values from -6 to 6
Outputs:
- pos_final: float32 [4, 16, 2, 3, 128], P('gx', 'gy', 'gz')
- vel_final: float32 [4, 16, 2, 3, 128], P('gx', 'gy', 'gz')
- grad_pos: float32 [4, 16, 2, 3, 128], P('gx', 'gy', 'gz')
- grad_vel: float32 [4, 16, 2, 3, 128], P('gx', 'gy', 'gz')
- grad_charge: float32 [4, 16, 2, 128], P('gx', 'gy', 'gz')
Inputs may be any that keep to these rules, and one draw needn't show every extreme that they name: `pair_list`: for k < pair_count[a, b, c] the two extended indices of slot k name blocks inside the global grid of 4 x 16 x 2 blocks, their coordinates differ by at most one in each dimension, and their smaller coordinate in each dimension lies in the device's own blocks; an unordered pair of blocks appears in at most one live slot over all devices. Slots at and past the count hold indices in range and are ignored. `pair_count`: some device has all 56 slots live in every draw.
All inputs are finite; a program needn't handle non-finite values.
Results may differ from a plain program's by a relative error of at most 0.00027.
Values sent between devices are 32-bit elements; how exact they have to be, the bound alone decides.
A program may use at most 64 MiB of HBM per device.

v0:
```python
import functools

import jax
import jax.numpy as jnp
from jax import lax
from jax.experimental import pallas as pl
from jax.experimental.pallas import tpu as pltpu
from jax.sharding import PartitionSpec as P

STEPS = 5


SOFT = 0.04
KAPPA = 2.0
TIME_STEP = 0.004
CHUNK = 16
BATCH = 8


def atom_params(charges, atom_types, atom_count, sigma_type, epsilon_type):
    type_total = sigma_type.shape[0]
    alive_mask = (
        lax.broadcasted_iota(jnp.int32, charges.shape, charges.ndim - 1) < atom_count[..., None]
    ).astype(jnp.float32)
    matches = (
        atom_types[..., None, :] == lax.broadcasted_iota(jnp.int32, (type_total, 1), 0)
    ).astype(jnp.float32)
    sigma_atom = jnp.sum(matches * sigma_type[:, None], axis=-2)
    depth_atom = jnp.sum(matches * epsilon_type[:, None], axis=-2)
    params = jnp.stack(
        [charges * alive_mask, 0.5 * sigma_atom, jnp.sqrt(depth_atom) * alive_mask, alive_mask],
        axis=-2,
    )
    return (alive_mask, params)


AXES = ("gx", "gy", "gz")
SIDES = [(x, y, z) for x in (0, 1) for y in (0, 1) for z in (0, 1)][1:]


def low_part(side, own):
    return tuple(pl.ds(0, 1 if d else n) for d, n in zip(side, own))


def rim_part(side, own):
    return tuple(pl.ds(n, 1) if d else pl.ds(0, n) for d, n in zip(side, own))


class Neighbours:
    def __init__(self, counts):
        self.counts = counts
        self.here = tuple(lax.axis_index(axis) for axis in AXES)

    def at(self, side, sign):
        return tuple(place + sign * step for place, step in zip(self.here, side))

    def exists(self, side, sign):
        found = None
        for place, step, count in zip(self.here, side, self.counts):
            if step:
                test = place < count - 1 if sign > 0 else place > 0
                found = test if found is None else jnp.logical_and(found, test)
        return found

    def greet(self):
        barrier = pltpu.get_barrier_semaphore()
        for sign in (1, -1):
            for side in SIDES:

                @pl.when(self.exists(side, sign))
                def _(side=side, sign=sign):
                    pl.semaphore_signal(
                        barrier,
                        inc=1,
                        device_id=self.at(side, sign),
                        device_id_type=pl.DeviceIdType.MESH,
                    )

        peers = sum(
            self.exists(side, sign).astype(jnp.int32) for sign in (1, -1) for side in SIDES
        )
        pl.semaphore_wait(barrier, peers)

    def copy(self, source, target, sems, index, side, sign):
        return pltpu.make_async_remote_copy(
            src_ref=source,
            dst_ref=target,
            send_sem=sems.at[0, index],
            recv_sem=sems.at[1, index],
            device_id=self.at(side, sign),
            device_id_type=pl.DeviceIdType.MESH,
        )


def returned_sum(near, part_ref, total_ref, landing, sems, own):
    def moved(index, side):
        return near.copy(
            part_ref.at[rim_part(side, own)], landing[index], sems, index, side, 1
        )

    for index, side in enumerate(SIDES):

        @pl.when(near.exists(side, 1))
        def _(index=index, side=side):
            moved(index, side).start()

    total_ref[...] = part_ref[tuple(pl.ds(0, n) for n in own)]
    for index, side in enumerate(SIDES):

        @pl.when(near.exists(side, -1))
        def _(index=index, side=side):
            moved(index, side).wait_recv()
            where = low_part(side, own)
            total_ref[where] = total_ref[where] + landing[index][...]

    def finish():
        for index, side in enumerate(SIDES):

            @pl.when(near.exists(side, 1))
            def _(index=index, side=side):
                moved(index, side).wait_send()

    return finish


def spread(near, value, ext_ref, sems, own):
    ext_ref[tuple(pl.ds(0, n) for n in own)] = value
    base = len(SIDES)

    def moved(index, side):
        return near.copy(
            ext_ref.at[low_part(side, own)],
            ext_ref.at[rim_part(side, own)],
            sems,
            base + index,
            side,
            -1,
        )

    for index, side in enumerate(SIDES):

        @pl.when(near.exists(side, -1))
        def _(index=index, side=side):
            moved(index, side).start()

    for index, side in enumerate(SIDES):

        @pl.when(jnp.logical_not(near.exists(side, 1)))
        def _(index=index, side=side):
            where = rim_part(side, own)
            shape = tuple(1 if d else n for d, n in zip(side, own)) + ext_ref.shape[3:]
            ext_ref[where] = jnp.zeros(shape, jnp.float32)

    def finish():
        for index, side in enumerate(SIDES):

            @pl.when(near.exists(side, 1))
            def _(index=index, side=side):
                moved(index, side).wait_recv()

        for index, side in enumerate(SIDES):

            @pl.when(near.exists(side, -1))
            def _(index=index, side=side):
                moved(index, side).wait_send()

    return finish


def first_kernel(counts, own, field_ref, ext_ref, sems):
    near = Neighbours(counts)
    near.greet()
    spread(near, field_ref[...], ext_ref, sems, own)()


def forward_kernel(counts, own, part, ext_old, vel, scale, ext_ref, vel_out, total, *rest):
    landing, sems = rest[:-1], rest[-1]
    near = Neighbours(counts)
    near.greet()
    sent = returned_sum(near, part, total, landing, sems, own)
    velocity = vel[...] + scale[...] * total[...]
    vel_out[...] = velocity
    position = ext_old[tuple(pl.ds(0, n) for n in own)] + TIME_STEP * velocity
    spread(near, position, ext_ref, sems, own)()
    sent()


def turn_kernel(
    counts, own, part, vel, vel_scale, gpos, gvel, scale,
    ext_ref, gpos_out, gvel_out, charge_out, vel_out, total, *rest,
):
    landing, sems = rest[:-1], rest[-1]
    near = Neighbours(counts)
    near.greet()
    sent = returned_sum(near, part, total, landing, sems, own)
    grad_position = gpos[...] + total[:, :, :, 3:6, :]
    grad_velocity = gvel[...] + TIME_STEP * grad_position
    finish = spread(near, scale[...] * grad_velocity, ext_ref, sems, own)
    gpos_out[...] = grad_position
    gvel_out[...] = grad_velocity
    charge_out[...] = total[:, :, :, 6:7, :]
    vel_out[...] = vel[...] + vel_scale[...] * total[:, :, :, 0:3, :]
    finish()
    sent()


def backward_kernel(
    counts, own, part, gpos, gvel, scale, charge,
    ext_ref, gpos_out, gvel_out, charge_out, total, *rest,
):
    landing, sems = rest[:-1], rest[-1]
    near = Neighbours(counts)
    near.greet()
    sent = returned_sum(near, part, total, landing, sems, own)
    grad_position = gpos[...] + total[:, :, :, 0:3, :]
    grad_velocity = gvel[...] + TIME_STEP * grad_position
    finish = spread(near, scale[...] * grad_velocity, ext_ref, sems, own)
    gpos_out[...] = grad_position
    gvel_out[...] = grad_velocity
    charge_out[...] = charge[...] + total[:, :, :, 3:4, :]
    finish()
    sent()


def last_kernel(counts, own, part, gpos, charge, alive, gpos_out, charge_out, total, *rest):
    landing, sems = rest[:-1], rest[-1]
    near = Neighbours(counts)
    near.greet()
    sent = returned_sum(near, part, total, landing, sems, own)
    gpos_out[...] = gpos[...] + total[:, :, :, 0:3, :]
    charge_out[...] = (charge[...] + total[:, :, :, 3:4, :]) * alive[...]
    sent()


def exchange(kernel, identity, own, rows_in, rows_out, *operands):
    counts = tuple(lax.axis_size(axis) for axis in AXES)
    per_block = operands[0].shape[-1]
    extended = tuple(n + 1 for n in own)
    outs = [
        jax.ShapeDtypeStruct((extended if rim else own) + (rows, per_block), jnp.float32)
        for rim, rows in rows_out
    ]
    scratch = []
    if rows_in:
        scratch.append(pltpu.VMEM(own + (rows_in, per_block), jnp.float32))
        for side in SIDES:
            shape = tuple(1 if d else n for d, n in zip(side, own))
            scratch.append(pltpu.VMEM(shape + (rows_in, per_block), jnp.float32))
    scratch.append(pltpu.SemaphoreType.DMA((2, 2 * len(SIDES))))
    vmem = pl.BlockSpec(memory_space=pltpu.VMEM)
    return pl.pallas_call(
        functools.partial(kernel, counts, own),
        out_shape=outs,
        in_specs=[vmem] * len(operands),
        out_specs=[vmem] * len(outs),
        scratch_shapes=scratch,
        compiler_params=pltpu.CompilerParams(
            collective_id=identity, has_side_effects=True, vmem_limit_bytes=4 * 1024 * 1024
        ),
    )(*operands)


def work_kernel(
    extent, per_block, pair_ref, live_ref, size_ref, item_ref, table_ref, shift_ref, count_ref
):
    extent_y, extent_z = extent

    def coords(index):
        return (index // (extent_y * extent_z), index // extent_z % extent_y, index % extent_z)

    slots = pair_ref.shape[1]
    steps = per_block // CHUNK

    def one_pair(slot, item):
        first = pair_ref[0, slot]
        second = pair_ref[1, slot]
        swap = size_ref[first] > size_ref[second]
        rows = jnp.where(swap, second, first)
        lanes = jnp.where(swap, first, second)
        table_ref[0, slot] = rows
        table_ref[1, slot] = lanes
        for axis, (one, two) in enumerate(zip(coords(rows), coords(lanes))):
            shift_ref[axis, slot] = (one - two).astype(jnp.float32)
        shift_ref[3, slot] = jnp.where(first == second, 0.5, 1.0).astype(jnp.float32)
        for step in range(steps):
            item_ref[item + step] = slot * steps + step
        return item + (size_ref[rows] + CHUNK - 1) // CHUNK

    items = lax.fori_loop(0, live_ref[0], one_pair, 0)
    for row in range(2):
        table_ref[row, slots] = 0
    for row in range(4):
        shift_ref[row, slots] = jnp.float32(0.0)
    for extra in range(BATCH - 1):
        item_ref[items + extra] = slots * steps
    count_ref[0] = (items + BATCH - 1) // BATCH


def work_list(extent, per_block, sizes, pair_list, pair_count):
    smem = pl.BlockSpec(memory_space=pltpu.SMEM)
    pairs = pair_list[0, 0, 0]
    slots = pairs.shape[1]
    steps = per_block // CHUNK
    return pl.pallas_call(
        functools.partial(work_kernel, extent[1:], per_block),
        out_shape=[
            jax.ShapeDtypeStruct(((slots + 1) * steps + BATCH,), jnp.int32),
            jax.ShapeDtypeStruct((2, slots + 1), jnp.int32),
            jax.ShapeDtypeStruct((4, slots + 1), jnp.float32),
            jax.ShapeDtypeStruct((1,), jnp.int32),
        ],
        in_specs=[smem] * 3,
        out_specs=[smem] * 4,
        compiler_params=pltpu.CompilerParams(vmem_limit_bytes=4 * 1024 * 1024),
    )(pairs, pair_count.reshape(1), sizes)


def sweep_kernel(force, adjoint, *refs):
    refs = list(refs)
    item_ref, table_ref, shift_ref, count_ref, pos_ref, par_ref = refs[:6]
    refs = refs[6:]
    cot_ref = refs.pop(0) if adjoint else None
    out_ref, state_ref, column_ref, row_ref, lane_ref = refs
    total, unused, per_block = pos_ref.shape
    rows_out = out_ref.shape[1]
    vectors = rows_out - 1 if adjoint else rows_out
    full = (CHUNK, per_block)
    steps = per_block // CHUNK

    for block in range(total):
        state_ref[block, 0:3, :] = pos_ref[block]
        state_ref[block, 3:7, :] = par_ref[block]
        if adjoint:
            state_ref[block, 8:11, :] = cot_ref[block]
    for block in range(total):
        column_ref[block] = state_ref[block].T

    def clear(block, carry):
        row_ref[block] = jnp.zeros((rows_out, per_block, per_block), jnp.float32)
        lane_ref[block] = jnp.zeros((rows_out, 8, per_block), jnp.float32)
        return carry

    lax.fori_loop(0, total, clear, 0)

    def item_terms(item):
        packed = item_ref[item]
        slot = packed // steps
        rows = table_ref[0, slot]
        lanes = table_ref[1, slot]
        start = pl.multiple_of((packed - slot * steps) * CHUNK, CHUNK)
        weight = shift_ref[3, slot]
        columns = column_ref[rows, pl.ds(start, CHUNK), :]

        def lane_row(part):
            return state_ref[lanes, part : part + 1, :]

        def row_column(part):
            return jnp.broadcast_to(columns[:, part : part + 1], full)

        lane_charge = lane_row(3) * (8.0 * weight)
        lane_depth = lane_row(5) * (24.0 * weight)
        d = [row_column(axis) - (lane_row(axis) - shift_ref[axis, slot]) for axis in range(3)]
        s = d[0] * d[0] + d[1] * d[1] + d[2] * d[2]
        sigma = row_column(4) + lane_row(4)
        square = sigma * sigma
        inverse = 1.0 / (s + square)
        t = square * inverse
        t3 = t * t * t
        soft = s + SOFT
        r = lax.rsqrt(soft)
        b = jnp.exp(-KAPPA * (soft * r)) * r
        c = jnp.maximum(1.0 - s, 0.0)
        cc = c * c
        p = c * inverse
        y = c * r
        row_charge = row_column(3)
        et = row_column(5) * lane_depth * t3
        below = t3 - 1.0
        twice = t3 + below
        half = 1.0 + 0.5 * r
        k1 = 3.0 + y * half
        charge_b = lane_charge * b
        qb = row_charge * charge_b
        g1 = cc * (et * (below + p * twice) + qb * k1)
        row_terms = []
        if force:
            row_terms += [g1 * d[axis] for axis in range(3)]
        if adjoint:
            h = p * (p * (7.0 * t3 - 2.0) + 3.0 * twice) + below
            k2 = y * (y * (1.0 + r * (1.5 + 0.75 * r)) + 6.0 * half) + 6.0
            k = -2.0 * c * (2.0 * et * h + qb * k2)
            delta = [row_column(8 + axis) - lane_row(8 + axis) for axis in range(3)]
            along = delta[0] * d[0] + delta[1] * d[1] + delta[2] * d[2]
            ka = k * along
            row_terms += [g1 * delta[axis] + ka * d[axis] for axis in range(3)]

        def folded(value):
            return functools.reduce(
                lambda one, two: one + two,
                [value[8 * group : 8 * group + 8] for group in range(CHUNK // 8)],
            )

        lane_terms = [-folded(value) for value in row_terms]
        if adjoint:
            m = cc * k1 * along
            row_terms.append(m * charge_b)
            lane_terms.append(folded(m * b * row_charge) * (8.0 * weight))
        return (rows, lanes, start, row_terms, lane_terms)

    def one_batch(batch, carry):
        found = [item_terms(batch * BATCH + index) for index in range(BATCH)]
        for rows, lanes, start, row_terms, lane_terms in found:
            where = pl.ds(start, CHUNK)
            old_rows = [row_ref[rows, part, where, :] for part in range(rows_out)]
            old_lanes = [lane_ref[lanes, part] for part in range(rows_out)]
            for part in range(rows_out):
                row_ref[rows, part, where, :] = old_rows[part] + row_terms[part]
                lane_ref[lanes, part] = old_lanes[part] + lane_terms[part]
        return carry

    lax.fori_loop(0, count_ref[0], one_batch, 0)

    which = lax.broadcasted_iota(jnp.int32, (per_block, 8), 1)
    for block in range(total):
        columns = jnp.zeros((per_block, 8), jnp.float32)
        for part in range(rows_out):
            summed = jnp.sum(row_ref[block, part], axis=1, keepdims=True)
            columns = jnp.where(which == part, summed, columns)
        turned = columns.T
        sums = [jnp.sum(lane_ref[block, part], axis=0, keepdims=True) for part in range(rows_out)]
        out_ref[block] = turned[0:rows_out] + jnp.concatenate(sums, axis=0)


def sweep(ext_pos, ext_par, work, ext_cot, force):
    extent = ext_pos.shape[:3]
    per_block = ext_pos.shape[-1]
    total = extent[0] * extent[1] * extent[2]
    adjoint = ext_cot is not None
    rows_out = (3 if force else 0) + (4 if adjoint else 0)
    operands = list(work) + [ext_pos.reshape(total, 3, per_block), ext_par]
    if adjoint:
        operands.append(ext_cot.reshape(total, 3, per_block))
    smem = pl.BlockSpec(memory_space=pltpu.SMEM)
    vmem = pl.BlockSpec(memory_space=pltpu.VMEM)
    height = 16 if adjoint else 8
    out = pl.pallas_call(
        functools.partial(sweep_kernel, force, adjoint),
        out_shape=jax.ShapeDtypeStruct((total, rows_out, per_block), jnp.float32),
        in_specs=[smem] * 4 + [vmem] * (len(operands) - 4),
        out_specs=vmem,
        scratch_shapes=[
            pltpu.VMEM((total, height, per_block), jnp.float32),
            pltpu.VMEM((total, per_block, height), jnp.float32),
            pltpu.VMEM((total, rows_out, per_block, per_block), jnp.float32),
            pltpu.VMEM((total, rows_out, 8, per_block), jnp.float32),
        ],
        compiler_params=pltpu.CompilerParams(vmem_limit_bytes=40 * 1024 * 1024),
    )(*operands)
    return out.reshape(extent + (rows_out, per_block))


def on_device(
    positions,
    velocities,
    charges,
    atom_types,
    atom_count,
    sigma_type,
    epsilon_type,
    masses,
    pair_list,
    pair_count,
    pos_cotangent,
    vel_cotangent,
):
    alive_mask, params = atom_params(charges, atom_types, atom_count, sigma_type, epsilon_type)
    inverse = (1.0 / masses)[..., None, :]
    half_step = 0.5 * TIME_STEP
    own = positions.shape[:3]
    per_block = positions.shape[-1]
    half_scale = jnp.broadcast_to(half_step * inverse, positions.shape)
    full_scale = jnp.broadcast_to(TIME_STEP * inverse, positions.shape)
    field = jnp.concatenate([positions, params, half_scale * vel_cotangent], axis=3)
    (extended,) = exchange(first_kernel, 1, own, 0, [(True, 10)], field)
    ext_par = extended[:, :, :, 3:7].reshape(-1, 4, per_block)
    last_cot = extended[:, :, :, 7:10]
    sizes = jnp.sum(ext_par[:, 3], axis=-1).astype(jnp.int32)
    work = work_list(extended.shape[:3], per_block, sizes, pair_list, pair_count)
    history = [extended[:, :, :, :3]]
    velocity = velocities
    for step_index in range(STEPS):
        part = sweep(history[-1], ext_par, work, None, True)
        scale = half_scale if step_index == 0 else full_scale
        ext_next, velocity = exchange(
            forward_kernel, 2, own, 3, [(True, 3), (False, 3)], part, history[-1], velocity, scale
        )
        history.append(ext_next)
    part = sweep(history[STEPS], ext_par, work, last_cot, True)
    ext_cot, grad_position, grad_velocity, charge_sum, velocity = exchange(
        turn_kernel,
        3,
        own,
        7,
        [(True, 3), (False, 3), (False, 3), (False, 1), (False, 3)],
        part,
        velocity,
        half_scale,
        pos_cotangent,
        vel_cotangent,
        full_scale,
    )
    for step_index in range(STEPS - 1, 0, -1):
        part = sweep(history[step_index], ext_par, work, ext_cot, False)
        scale = full_scale if step_index > 1 else half_scale
        ext_cot, grad_position, grad_velocity, charge_sum = exchange(
            backward_kernel,
            4,
            own,
            4,
            [(True, 3), (False, 3), (False, 3), (False, 1)],
            part,
            grad_position,
            grad_velocity,
            scale,
            charge_sum,
        )
    part = sweep(history[0], ext_par, work, ext_cot, False)
    grad_position, charge_sum = exchange(
        last_kernel,
        5,
        own,
        4,
        [(False, 3), (False, 1)],
        part,
        grad_position,
        charge_sum,
        alive_mask[..., None, :],
    )
    position = history[STEPS][: own[0], : own[1], : own[2]]
    return (position, velocity, grad_position, grad_velocity, charge_sum[:, :, :, 0])


def solution(mesh):
    in_specs = (
        P("gx", "gy", "gz", None, None),
        P("gx", "gy", "gz", None, None),
        P("gx", "gy", "gz", None),
        P("gx", "gy", "gz", None),
        P("gx", "gy", "gz"),
        P(),
        P(),
        P("gx", "gy", "gz", None),
        P("gx", "gy", "gz", None, None),
        P("gx", "gy", "gz"),
        P("gx", "gy", "gz", None, None),
        P("gx", "gy", "gz", None, None),
    )
    out_specs = (
        P("gx", "gy", "gz", None, None),
        P("gx", "gy", "gz", None, None),
        P("gx", "gy", "gz", None, None),
        P("gx", "gy", "gz", None, None),
        P("gx", "gy", "gz", None),
    )
    return jax.shard_map(
        on_device, mesh=mesh, in_specs=in_specs, out_specs=out_specs, check_vma=False
    )
```

profile of v0, /device:TPU:11, one launch (start us, length us, event | category | flops | bytes accessed | tf_op | source)
XLA Modules:
  0.0 256.6 jit_solution(16150331513711464181)
XLA Ops:
  5.1 6.1 %shard_map.158 = f32[2,5,2,10,128]{4,3,2,1,0:T(8,128)S(1)} custom-call(f32[1,4,1,10,128]{4,3,2,1,0:T(8,128)S(1)} %concatenate.3.field_ref), custom_call_target="tpu_custom_call" | custom-call | tf_op jit(solution)/shard_map/pallas_call | solution.py:251
  12.2 2.2 shard_map.159
  14.5 7.0 %shard_map.160 = f32[20,3,128]{2,1,0:T(4,128)S(1)} custom-call(s32[464]{0:T(512)S(1)} %get-tuple-element.42.refs_0_, s32[2,57]{1,0:T(2,128)S(1)} %get-tuple-element.43.refs_1_, f32[4,57]{1,0:T(4,128)S(1)} %get-tuple-element.44.refs_2_, s32[1]{0:T(128)} %get-tuple-element.45.refs_3_, f32[20,3,128]{2,1,0:T(4,128)S(1)} %bitcast.50, f32[20,4,128]{2,1,0:T(4,128)S(1)} %bitcast.39), custom_call_target="tpu_custom_call" | custom-call | tf_op jit(solution)/shard_map/pallas_call | solution.py:446
  21.4 14.0 %shard_map.161 = (f32[2,5,2,3,128]{4,3,2,1,0:T(4,128)S(1)}, f32[1,4,1,3,128]{4,3,2,1,0:T(4,128)S(1)}) custom-call(f32[2,5,2,3,128]{4,3,2,1,0:T(4,128)S(1)} %bitcast.63, f32[2,5,2,3,128]{4,3,2,1,0:T(4,128)S(1)} %get-tuple-element.94.ext_old, f32[1,4,1,3,128]{4,3,2,1,0:T(4,128)S(1)} %copy.31.vel, f32[1,4,1,3,128]{4,3,2,1,0:T(4,128)S(1)} %broadcast_in_dim.4.scale.vel_scale), custom_call_target="tpu_custom_call" | custom-call | tf_op jit(solution)/shard_map/pallas_call | solution.py:251
  35.5 7.0 %shard_map.162 = f32[20,3,128]{2,1,0:T(4,128)S(1)} custom-call(s32[464]{0:T(512)S(1)} %get-tuple-element.42.refs_0_, s32[2,57]{1,0:T(2,128)S(1)} %get-tuple-element.43.refs_1_, f32[4,57]{1,0:T(4,128)S(1)} %get-tuple-element.44.refs_2_, s32[1]{0:T(128)} %get-tuple-element.45.refs_3_, f32[20,3,128]{2,1,0:T(4,128)S(1)} %bitcast.52, f32[20,4,128]{2,1,0:T(4,128)S(1)} %bitcast.40), custom_call_target="tpu_custom_call" | custom-call | tf_op jit(solution)/shard_map/pallas_call | solution.py:446
  42.4 12.3 %shard_map.163 = (f32[2,5,2,3,128]{4,3,2,1,0:T(4,128)S(1)}, f32[1,4,1,3,128]{4,3,2,1,0:T(4,128)S(1)}) custom-call(f32[2,5,2,3,128]{4,3,2,1,0:T(4,128)S(1)} %bitcast.62, f32[2,5,2,3,128]{4,3,2,1,0:T(4,128)S(1)} %get-tuple-element.46.ext_old, f32[1,4,1,3,128]{4,3,2,1,0:T(4,128)S(1)} %get-tuple-element.47.vel, f32[1,4,1,3,128]{4,3,2,1,0:T(4,128)S(1)} %broadcast_in_dim.5.scale), custom_call_target="tpu_custom_call" | custom-call | tf_op jit(solution)/shard_map/pallas_call | solution.py:251
  54.7 7.0 %shard_map.164 = f32[20,3,128]{2,1,0:T(4,128)S(1)} custom-call(s32[464]{0:T(512)S(1)} %get-tuple-element.42.refs_0_, s32[2,57]{1,0:T(2,128)S(1)} %get-tuple-element.43.refs_1_, f32[4,57]{1,0:T(4,128)S(1)} %get-tuple-element.44.refs_2_, s32[1]{0:T(128)} %get-tuple-element.45.refs_3_, f32[20,3,128]{2,1,0:T(4,128)S(1)} %bitcast.54, f32[20,4,128]{2,1,0:T(4,128)S(1)} %bitcast.41), custom_call_target="tpu_custom_call" | custom-call | tf_op jit(solution)/shard_map/pallas_call | solution.py:446
  61.7 12.3 %shard_map.165 = (f32[2,5,2,3,128]{4,3,2,1,0:T(4,128)S(1)}, f32[1,4,1,3,128]{4,3,2,1,0:T(4,128)S(1)}) custom-call(f32[2,5,2,3,128]{4,3,2,1,0:T(4,128)S(1)} %bitcast.64, f32[2,5,2,3,128]{4,3,2,1,0:T(4,128)S(1)} %get-tuple-element.48.ext_old, f32[1,4,1,3,128]{4,3,2,1,0:T(4,128)S(1)} %get-tuple-element.49.vel, f32[1,4,1,3,128]{4,3,2,1,0:T(4,128)S(1)} %broadcast_in_dim.5.scale), custom_call_target="tpu_custom_call" | custom-call | tf_op jit(solution)/shard_map/pallas_call | solution.py:251
  74.0 7.0 %shard_map.166 = f32[20,3,128]{2,1,0:T(4,128)S(1)} custom-call(s32[464]{0:T(512)S(1)} %get-tuple-element.42.refs_0_, s32[2,57]{1,0:T(2,128)S(1)} %get-tuple-element.43.refs_1_, f32[4,57]{1,0:T(4,128)S(1)} %get-tuple-element.44.refs_2_, s32[1]{0:T(128)} %get-tuple-element.45.refs_3_, f32[20,3,128]{2,1,0:T(4,128)S(1)} %bitcast.56, f32[20,4,128]{2,1,0:T(4,128)S(1)} %bitcast.42), custom_call_target="tpu_custom_call" | custom-call | tf_op jit(solution)/shard_map/pallas_call | solution.py:446
  81.0 12.3 %shard_map.167 = (f32[2,5,2,3,128]{4,3,2,1,0:T(4,128)S(1)}, f32[1,4,1,3,128]{4,3,2,1,0:T(4,128)S(1)}) custom-call(f32[2,5,2,3,128]{4,3,2,1,0:T(4,128)S(1)} %bitcast.65, f32[2,5,2,3,128]{4,3,2,1,0:T(4,128)S(1)} %get-tuple-element.50.ext_old, f32[1,4,1,3,128]{4,3,2,1,0:T(4,128)S(1)} %get-tuple-element.51.vel, f32[1,4,1,3,128]{4,3,2,1,0:T(4,128)S(1)} %broadcast_in_dim.5.scale), custom_call_target="tpu_custom_call" | custom-call | tf_op jit(solution)/shard_map/pallas_call | solution.py:251
  93.3 7.0 %shard_map.168 = f32[20,3,128]{2,1,0:T(4,128)S(1)} custom-call(s32[464]{0:T(512)S(1)} %get-tuple-element.42.refs_0_, s32[2,57]{1,0:T(2,128)S(1)} %get-tuple-element.43.refs_1_, f32[4,57]{1,0:T(4,128)S(1)} %get-tuple-element.44.refs_2_, s32[1]{0:T(128)} %get-tuple-element.45.refs_3_, f32[20,3,128]{2,1,0:T(4,128)S(1)} %bitcast.58, f32[20,4,128]{2,1,0:T(4,128)S(1)} %bitcast.43), custom_call_target="tpu_custom_call" | custom-call | tf_op jit(solution)/shard_map/pallas_call | solution.py:446
  100.2 12.3 %shard_map.169 = (f32[2,5,2,3,128]{4,3,2,1,0:T(4,128)S(1)}, f32[1,4,1,3,128]{4,3,2,1,0:T(4,128)S(1)}) custom-call(f32[2,5,2,3,128]{4,3,2,1,0:T(4,128)S(1)} %bitcast.66, f32[2,5,2,3,128]{4,3,2,1,0:T(4,128)S(1)} %get-tuple-element.52.ext_old, f32[1,4,1,3,128]{4,3,2,1,0:T(4,128)S(1)} %get-tuple-element.53.vel, f32[1,4,1,3,128]{4,3,2,1,0:T(4,128)S(1)} %broadcast_in_dim.5.scale), custom_call_target="tpu_custom_call" | custom-call | tf_op jit(solution)/shard_map/pallas_call | solution.py:251
  113.2 10.7 %shard_map.170 = f32[20,7,128]{2,1,0:T(8,128)S(1)} custom-call(s32[464]{0:T(512)S(1)} %get-tuple-element.42.refs_0_, s32[2,57]{1,0:T(2,128)S(1)} %get-tuple-element.43.refs_1_, f32[4,57]{1,0:T(4,128)S(1)} %get-tuple-element.44.refs_2_, s32[1]{0:T(128)} %get-tuple-element.45.refs_3_, f32[20,3,128]{2,1,0:T(4,128)S(1)} %bitcast.72, f32[20,4,128]{2,1,0:T(4,128)S(1)} %bitcast.44, ...), custom_call_target="tpu_custom_call" | custom-call | tf_op jit(solution)/shard_map/pallas_call | solution.py:446
  123.9 15.4 %shard_map.171 = (f32[2,5,2,3,128]{4,3,2,1,0:T(4,128)S(1)}, f32[1,4,1,3,128]{4,3,2,1,0:T(4,128)S(1)}, f32[1,4,1,3,128]{4,3,2,1,0:T(4,128)S(1)}, f32[1,4,1,1,128]{4,3,2,1,0:T(1,128)S(1)}, f32[1,4,1,3,128]{4,3,2,1,0:T(4,128)S(1)}) custom-call(f32[2,5,2,7,128]{4,3,2,1,0:T(8,128)S(1)} %bitcast.60, f32[1,4,1,3,128]{4,3,2,1,0:T(4,128)S(1)} %get-tuple-element.55.vel, ...), custom_call_target="tpu_custom_call" | custom-call | tf_op jit(solution)/shard_map/pallas_call | solution.py:251
  139.9 8.9 %shard_map.172 = f32[20,4,128]{2,1,0:T(4,128)S(1)} custom-call(s32[464]{0:T(512)S(1)} %get-tuple-element.42.refs_0_, s32[2,57]{1,0:T(2,128)S(1)} %get-tuple-element.43.refs_1_, f32[4,57]{1,0:T(4,128)S(1)} %get-tuple-element.44.refs_2_, s32[1]{0:T(128)} %get-tuple-element.45.refs_3_, f32[20,3,128]{2,1,0:T(4,128)S(1)} %bitcast.59, f32[20,4,128]{2,1,0:T(4,128)S(1)} %bitcast.45, ...), custom_call_target="tpu_custom_call" | custom-call | tf_op jit(solution)/shard_map/pallas_call | solution.py:446
  148.8 14.4 %shard_map.173 = (f32[2,5,2,3,128]{4,3,2,1,0:T(4,128)S(1)}, f32[1,4,1,3,128]{4,3,2,1,0:T(4,128)S(1)}, f32[1,4,1,3,128]{4,3,2,1,0:T(4,128)S(1)}, f32[1,4,1,1,128]{4,3,2,1,0:T(1,128)S(1)}) custom-call(f32[2,5,2,4,128]{4,3,2,1,0:T(4,128)S(1)} %bitcast.69, f32[1,4,1,3,128]{4,3,2,1,0:T(4,128)S(1)} %get-tuple-element.58.gpos, ...), custom_call_target="tpu_custom_call" | custom-call | tf_op jit(solution)/shard_map/pallas_call | solution.py:251
  163.2 8.9 %shard_map.174 = f32[20,4,128]{2,1,0:T(4,128)S(1)} custom-call(s32[464]{0:T(512)S(1)} %get-tuple-element.42.refs_0_, s32[2,57]{1,0:T(2,128)S(1)} %get-tuple-element.43.refs_1_, f32[4,57]{1,0:T(4,128)S(1)} %get-tuple-element.44.refs_2_, s32[1]{0:T(128)} %get-tuple-element.45.refs_3_, f32[20,3,128]{2,1,0:T(4,128)S(1)} %bitcast.57, f32[20,4,128]{2,1,0:T(4,128)S(1)} %bitcast.46, ...), custom_call_target="tpu_custom_call" | custom-call | tf_op jit(solution)/shard_map/pallas_call | solution.py:446
  172.1 14.6 %shard_map.175 = (f32[2,5,2,3,128]{4,3,2,1,0:T(4,128)S(1)}, f32[1,4,1,3,128]{4,3,2,1,0:T(4,128)S(1)}, f32[1,4,1,3,128]{4,3,2,1,0:T(4,128)S(1)}, f32[1,4,1,1,128]{4,3,2,1,0:T(1,128)S(1)}) custom-call(f32[2,5,2,4,128]{4,3,2,1,0:T(4,128)S(1)} %bitcast.70, f32[1,4,1,3,128]{4,3,2,1,0:T(4,128)S(1)} %get-tuple-element.62.gpos, ...), custom_call_target="tpu_custom_call" | custom-call | tf_op jit(solution)/shard_map/pallas_call | solution.py:251
  186.7 8.9 %shard_map.176 = f32[20,4,128]{2,1,0:T(4,128)S(1)} custom-call(s32[464]{0:T(512)S(1)} %get-tuple-element.42.refs_0_, s32[2,57]{1,0:T(2,128)S(1)} %get-tuple-element.43.refs_1_, f32[4,57]{1,0:T(4,128)S(1)} %get-tuple-element.44.refs_2_, s32[1]{0:T(128)} %get-tuple-element.45.refs_3_, f32[20,3,128]{2,1,0:T(4,128)S(1)} %bitcast.55, f32[20,4,128]{2,1,0:T(4,128)S(1)} %bitcast.47, ...), custom_call_target="tpu_custom_call" | custom-call | tf_op jit(solution)/shard_map/pallas_call | solution.py:446
  195.5 14.6 %shard_map.177 = (f32[2,5,2,3,128]{4,3,2,1,0:T(4,128)S(1)}, f32[1,4,1,3,128]{4,3,2,1,0:T(4,128)S(1)}, f32[1,4,1,3,128]{4,3,2,1,0:T(4,128)S(1)}, f32[1,4,1,1,128]{4,3,2,1,0:T(1,128)S(1)}) custom-call(f32[2,5,2,4,128]{4,3,2,1,0:T(4,128)S(1)} %bitcast.67, f32[1,4,1,3,128]{4,3,2,1,0:T(4,128)S(1)} %get-tuple-element.66.gpos, ...), custom_call_target="tpu_custom_call" | custom-call | tf_op jit(solution)/shard_map/pallas_call | solution.py:251
  210.1 9.1 %shard_map.178 = f32[20,4,128]{2,1,0:T(4,128)S(1)} custom-call(s32[464]{0:T(512)S(1)} %get-tuple-element.42.refs_0_, s32[2,57]{1,0:T(2,128)S(1)} %get-tuple-element.43.refs_1_, f32[4,57]{1,0:T(4,128)S(1)} %get-tuple-element.44.refs_2_, s32[1]{0:T(128)} %get-tuple-element.45.refs_3_, f32[20,3,128]{2,1,0:T(4,128)S(1)} %bitcast.53, f32[20,4,128]{2,1,0:T(4,128)S(1)} %bitcast.48, ...), custom_call_target="tpu_custom_call" | custom-call | tf_op jit(solution)/shard_map/pallas_call | solution.py:446
  219.2 14.6 %shard_map.179 = (f32[2,5,2,3,128]{4,3,2,1,0:T(4,128)S(1)}, f32[1,4,1,3,128]{4,3,2,1,0:T(4,128)S(1)}, f32[1,4,1,3,128]{4,3,2,1,0:T(4,128)S(1)}, f32[1,4,1,1,128]{4,3,2,1,0:T(1,128)S(1)}) custom-call(f32[2,5,2,4,128]{4,3,2,1,0:T(4,128)S(1)} %bitcast.68, f32[1,4,1,3,128]{4,3,2,1,0:T(4,128)S(1)} %get-tuple-element.70.gpos, ...), custom_call_target="tpu_custom_call" | custom-call | tf_op jit(solution)/shard_map/pallas_call | solution.py:251
  233.7 8.9 %shard_map.180 = f32[20,4,128]{2,1,0:T(4,128)S(1)} custom-call(s32[464]{0:T(512)S(1)} %get-tuple-element.42.refs_0_, s32[2,57]{1,0:T(2,128)S(1)} %get-tuple-element.43.refs_1_, f32[4,57]{1,0:T(4,128)S(1)} %get-tuple-element.44.refs_2_, s32[1]{0:T(128)} %get-tuple-element.45.refs_3_, f32[20,3,128]{2,1,0:T(4,128)S(1)} %bitcast.51, f32[20,4,128]{2,1,0:T(4,128)S(1)} %bitcast.49, ...), custom_call_target="tpu_custom_call" | custom-call | tf_op jit(solution)/shard_map/pallas_call | solution.py:446
  242.6 12.2 %shard_map.181 = (f32[1,4,1,3,128]{4,3,2,1,0:T(4,128)S(1)}, f32[1,4,1,1,128]{4,3,2,1,0:T(1,128)S(1)}) custom-call(f32[2,5,2,4,128]{4,3,2,1,0:T(4,128)S(1)} %bitcast.71, f32[1,4,1,3,128]{4,3,2,1,0:T(4,128)S(1)} %get-tuple-element.74.gpos, f32[1,4,1,1,128]{4,3,2,1,0:T(1,128)S(1)} %get-tuple-element.75.charge, f32[1,4,1,1,128]{4,3,2,1,0:T(1,128)S(1)} %compare_convert_fusion.alive), custom_call_target="tpu_custom_call" | custom-call | tf_op jit(solution)/shard_map/pallas_call | solution.py:251
  (45 shorter events, 7.7 us)
Async XLA Ops:
  2.0 0.7 copy-start.7
  2.0 0.7 copy-start.4
  2.7 0.7 copy-start.5
  2.7 0.7 copy-start.8
  2.7 0.7 copy-start.9
  3.6 0.7 copy-start.6
  4.3 0.7 copy-start.3
  11.5 0.7 copy-start
  14.4 7.0 %copy-start.1 = (f32[1,4,1,3,128]{4,2,3,1,0:T(1,128)S(1)}, f32[1,4,1,3,128]{4,2,3,1,0:T(1,128)}, u32[]{:S(2)}) copy-start(f32[1,4,1,3,128]{4,2,3,1,0:T(1,128)} %param.13) | copy-start | bytes 18436
  113.2 10.7 %copy-start.2 = (f32[1,4,1,3,128]{4,2,3,1,0:T(1,128)S(1)}, f32[1,4,1,3,128]{4,2,3,1,0:T(1,128)}, u32[]{:S(2)}) copy-start(f32[1,4,1,3,128]{4,2,3,1,0:T(1,128)} %param.22) | copy-start | bytes 18436
where the time goes:
time: 257 us
  Pallas kernels  247 us (96%)
  local copies, waits for them, and re-layouts  7.18 us (3%)
    pallas_call x12, Pallas kernels, exchange(): pl.pallas_call(functools.partial(kernel, counts, own), out_shape=outs, in...  155 us
    pallas_call x11, Pallas kernels, sweep(): pl.pallas_call(functools.partial(sweep_kernel, force, adjoint), out_shape...  90.1 us
    unnamed x28, local copies, waits for them, and re-layouts  7.01 us

commit v1 on v0

--- a/solution.py
+++ b/solution.py
@@ -1,4 +1,5 @@
 import functools
+import math
 
 import jax
 import jax.numpy as jnp
@@ -12,6 +13,7 @@
 
 SOFT = 0.04
 KAPPA = 2.0
+EXPONENT = -KAPPA / math.log(2.0)
 TIME_STEP = 0.004
 CHUNK = 16
 BATCH = 8
@@ -35,7 +37,9 @@
 
 
 AXES = ("gx", "gy", "gz")
-SIDES = [(x, y, z) for x in (0, 1) for y in (0, 1) for z in (0, 1)][1:]
+SIDES = sorted(
+    [(x, y, z) for x in (0, 1) for y in (0, 1) for z in (0, 1)][1:], key=sum, reverse=True
+)
 
 
 def low_part(side, own):
@@ -368,7 +372,7 @@
         t3 = t * t * t
         soft = s + SOFT
         r = lax.rsqrt(soft)
-        b = jnp.exp(-KAPPA * (soft * r)) * r
+        b = jnp.exp2(EXPONENT * (soft * r)) * r
         c = jnp.maximum(1.0 - s, 0.0)
         cc = c * c
         p = c * inverse

time: 257 us -> 255 us (level); the launches traced: 257 us -> 260 us
  Pallas kernels: 247 us -> 251 us
    pallas_call x12, Pallas kernels: 155 us -> 169 us  [exchange(): pl.pallas_call(functools.partial(kernel, counts, own), out_shape=outs, in...]
    pallas_call x11, Pallas kernels: 90.1 us -> 79.7 us  [sweep(): pl.pallas_call(functools.partial(sweep_kernel, force, adjoint), out_shape...]
where the time goes in v1:
time: 255 us; the launch traced here: 260 us
  Pallas kernels  251 us (98%)
  local copies, waits for them, and re-layouts  7.18 us (3%)
    pallas_call x12, Pallas kernels, exchange(): pl.pallas_call(functools.partial(kernel, counts, own), out_shape=outs, in...  169 us
    pallas_call x11, Pallas kernels, sweep(): pl.pallas_call(functools.partial(sweep_kernel, force, adjoint), out_shape...  79.7 us
    unnamed x28, local copies, waits for them, and re-layouts  7.01 us

profile of v1, /device:TPU:11, one launch (start us, length us, event | category | flops | bytes accessed | tf_op | source)
XLA Modules:
  0.0 260.0 jit_solution(2525631114482549282)
XLA Ops:
  5.1 6.2 %shard_map.158 = f32[2,5,2,10,128]{4,3,2,1,0:T(8,128)S(1)} custom-call(f32[1,4,1,10,128]{4,3,2,1,0:T(8,128)S(1)} %concatenate.3.field_ref), custom_call_target="tpu_custom_call" | custom-call | tf_op jit(solution)/shard_map/pallas_call | solution.py:255
  12.3 2.2 shard_map.159
  14.5 6.2 %shard_map.160 = f32[20,3,128]{2,1,0:T(4,128)S(1)} custom-call(s32[464]{0:T(512)S(1)} %get-tuple-element.42.refs_0_, s32[2,57]{1,0:T(2,128)S(1)} %get-tuple-element.43.refs_1_, f32[4,57]{1,0:T(4,128)S(1)} %get-tuple-element.44.refs_2_, s32[1]{0:T(128)} %get-tuple-element.45.refs_3_, f32[20,3,128]{2,1,0:T(4,128)S(1)} %bitcast.50, f32[20,4,128]{2,1,0:T(4,128)S(1)} %bitcast.39), custom_call_target="tpu_custom_call" | custom-call | tf_op jit(solution)/shard_map/pallas_call | solution.py:450
  20.7 14.9 %shard_map.161 = (f32[2,5,2,3,128]{4,3,2,1,0:T(4,128)S(1)}, f32[1,4,1,3,128]{4,3,2,1,0:T(4,128)S(1)}) custom-call(f32[2,5,2,3,128]{4,3,2,1,0:T(4,128)S(1)} %bitcast.63, f32[2,5,2,3,128]{4,3,2,1,0:T(4,128)S(1)} %get-tuple-element.94.ext_old, f32[1,4,1,3,128]{4,3,2,1,0:T(4,128)S(1)} %copy.31.vel, f32[1,4,1,3,128]{4,3,2,1,0:T(4,128)S(1)} %broadcast_in_dim.4.scale.vel_scale), custom_call_target="tpu_custom_call" | custom-call | tf_op jit(solution)/shard_map/pallas_call | solution.py:255
  35.6 6.2 %shard_map.162 = f32[20,3,128]{2,1,0:T(4,128)S(1)} custom-call(s32[464]{0:T(512)S(1)} %get-tuple-element.42.refs_0_, s32[2,57]{1,0:T(2,128)S(1)} %get-tuple-element.43.refs_1_, f32[4,57]{1,0:T(4,128)S(1)} %get-tuple-element.44.refs_2_, s32[1]{0:T(128)} %get-tuple-element.45.refs_3_, f32[20,3,128]{2,1,0:T(4,128)S(1)} %bitcast.52, f32[20,4,128]{2,1,0:T(4,128)S(1)} %bitcast.40), custom_call_target="tpu_custom_call" | custom-call | tf_op jit(solution)/shard_map/pallas_call | solution.py:450
  41.8 13.4 %shard_map.163 = (f32[2,5,2,3,128]{4,3,2,1,0:T(4,128)S(1)}, f32[1,4,1,3,128]{4,3,2,1,0:T(4,128)S(1)}) custom-call(f32[2,5,2,3,128]{4,3,2,1,0:T(4,128)S(1)} %bitcast.62, f32[2,5,2,3,128]{4,3,2,1,0:T(4,128)S(1)} %get-tuple-element.46.ext_old, f32[1,4,1,3,128]{4,3,2,1,0:T(4,128)S(1)} %get-tuple-element.47.vel, f32[1,4,1,3,128]{4,3,2,1,0:T(4,128)S(1)} %broadcast_in_dim.5.scale), custom_call_target="tpu_custom_call" | custom-call | tf_op jit(solution)/shard_map/pallas_call | solution.py:255
  55.3 6.2 %shard_map.164 = f32[20,3,128]{2,1,0:T(4,128)S(1)} custom-call(s32[464]{0:T(512)S(1)} %get-tuple-element.42.refs_0_, s32[2,57]{1,0:T(2,128)S(1)} %get-tuple-element.43.refs_1_, f32[4,57]{1,0:T(4,128)S(1)} %get-tuple-element.44.refs_2_, s32[1]{0:T(128)} %get-tuple-element.45.refs_3_, f32[20,3,128]{2,1,0:T(4,128)S(1)} %bitcast.54, f32[20,4,128]{2,1,0:T(4,128)S(1)} %bitcast.41), custom_call_target="tpu_custom_call" | custom-call | tf_op jit(solution)/shard_map/pallas_call | solution.py:450
  61.5 13.4 %shard_map.165 = (f32[2,5,2,3,128]{4,3,2,1,0:T(4,128)S(1)}, f32[1,4,1,3,128]{4,3,2,1,0:T(4,128)S(1)}) custom-call(f32[2,5,2,3,128]{4,3,2,1,0:T(4,128)S(1)} %bitcast.64, f32[2,5,2,3,128]{4,3,2,1,0:T(4,128)S(1)} %get-tuple-element.48.ext_old, f32[1,4,1,3,128]{4,3,2,1,0:T(4,128)S(1)} %get-tuple-element.49.vel, f32[1,4,1,3,128]{4,3,2,1,0:T(4,128)S(1)} %broadcast_in_dim.5.scale), custom_call_target="tpu_custom_call" | custom-call | tf_op jit(solution)/shard_map/pallas_call | solution.py:255
  74.9 6.2 %shard_map.166 = f32[20,3,128]{2,1,0:T(4,128)S(1)} custom-call(s32[464]{0:T(512)S(1)} %get-tuple-element.42.refs_0_, s32[2,57]{1,0:T(2,128)S(1)} %get-tuple-element.43.refs_1_, f32[4,57]{1,0:T(4,128)S(1)} %get-tuple-element.44.refs_2_, s32[1]{0:T(128)} %get-tuple-element.45.refs_3_, f32[20,3,128]{2,1,0:T(4,128)S(1)} %bitcast.56, f32[20,4,128]{2,1,0:T(4,128)S(1)} %bitcast.42), custom_call_target="tpu_custom_call" | custom-call | tf_op jit(solution)/shard_map/pallas_call | solution.py:450
  81.1 13.4 %shard_map.167 = (f32[2,5,2,3,128]{4,3,2,1,0:T(4,128)S(1)}, f32[1,4,1,3,128]{4,3,2,1,0:T(4,128)S(1)}) custom-call(f32[2,5,2,3,128]{4,3,2,1,0:T(4,128)S(1)} %bitcast.65, f32[2,5,2,3,128]{4,3,2,1,0:T(4,128)S(1)} %get-tuple-element.50.ext_old, f32[1,4,1,3,128]{4,3,2,1,0:T(4,128)S(1)} %get-tuple-element.51.vel, f32[1,4,1,3,128]{4,3,2,1,0:T(4,128)S(1)} %broadcast_in_dim.5.scale), custom_call_target="tpu_custom_call" | custom-call | tf_op jit(solution)/shard_map/pallas_call | solution.py:255
  94.6 6.2 %shard_map.168 = f32[20,3,128]{2,1,0:T(4,128)S(1)} custom-call(s32[464]{0:T(512)S(1)} %get-tuple-element.42.refs_0_, s32[2,57]{1,0:T(2,128)S(1)} %get-tuple-element.43.refs_1_, f32[4,57]{1,0:T(4,128)S(1)} %get-tuple-element.44.refs_2_, s32[1]{0:T(128)} %get-tuple-element.45.refs_3_, f32[20,3,128]{2,1,0:T(4,128)S(1)} %bitcast.58, f32[20,4,128]{2,1,0:T(4,128)S(1)} %bitcast.43), custom_call_target="tpu_custom_call" | custom-call | tf_op jit(solution)/shard_map/pallas_call | solution.py:450
  100.8 13.4 %shard_map.169 = (f32[2,5,2,3,128]{4,3,2,1,0:T(4,128)S(1)}, f32[1,4,1,3,128]{4,3,2,1,0:T(4,128)S(1)}) custom-call(f32[2,5,2,3,128]{4,3,2,1,0:T(4,128)S(1)} %bitcast.66, f32[2,5,2,3,128]{4,3,2,1,0:T(4,128)S(1)} %get-tuple-element.52.ext_old, f32[1,4,1,3,128]{4,3,2,1,0:T(4,128)S(1)} %get-tuple-element.53.vel, f32[1,4,1,3,128]{4,3,2,1,0:T(4,128)S(1)} %broadcast_in_dim.5.scale), custom_call_target="tpu_custom_call" | custom-call | tf_op jit(solution)/shard_map/pallas_call | solution.py:255
  114.8 9.5 %shard_map.170 = f32[20,7,128]{2,1,0:T(8,128)S(1)} custom-call(s32[464]{0:T(512)S(1)} %get-tuple-element.42.refs_0_, s32[2,57]{1,0:T(2,128)S(1)} %get-tuple-element.43.refs_1_, f32[4,57]{1,0:T(4,128)S(1)} %get-tuple-element.44.refs_2_, s32[1]{0:T(128)} %get-tuple-element.45.refs_3_, f32[20,3,128]{2,1,0:T(4,128)S(1)} %bitcast.72, f32[20,4,128]{2,1,0:T(4,128)S(1)} %bitcast.44, ...), custom_call_target="tpu_custom_call" | custom-call | tf_op jit(solution)/shard_map/pallas_call | solution.py:450
  124.4 16.7 %shard_map.171 = (f32[2,5,2,3,128]{4,3,2,1,0:T(4,128)S(1)}, f32[1,4,1,3,128]{4,3,2,1,0:T(4,128)S(1)}, f32[1,4,1,3,128]{4,3,2,1,0:T(4,128)S(1)}, f32[1,4,1,1,128]{4,3,2,1,0:T(1,128)S(1)}, f32[1,4,1,3,128]{4,3,2,1,0:T(4,128)S(1)}) custom-call(f32[2,5,2,7,128]{4,3,2,1,0:T(8,128)S(1)} %bitcast.60, f32[1,4,1,3,128]{4,3,2,1,0:T(4,128)S(1)} %get-tuple-element.55.vel, ...), custom_call_target="tpu_custom_call" | custom-call | tf_op jit(solution)/shard_map/pallas_call | solution.py:255
  141.7 7.8 %shard_map.172 = f32[20,4,128]{2,1,0:T(4,128)S(1)} custom-call(s32[464]{0:T(512)S(1)} %get-tuple-element.42.refs_0_, s32[2,57]{1,0:T(2,128)S(1)} %get-tuple-element.43.refs_1_, f32[4,57]{1,0:T(4,128)S(1)} %get-tuple-element.44.refs_2_, s32[1]{0:T(128)} %get-tuple-element.45.refs_3_, f32[20,3,128]{2,1,0:T(4,128)S(1)} %bitcast.59, f32[20,4,128]{2,1,0:T(4,128)S(1)} %bitcast.45, ...), custom_call_target="tpu_custom_call" | custom-call | tf_op jit(solution)/shard_map/pallas_call | solution.py:450
  149.5 16.3 %shard_map.173 = (f32[2,5,2,3,128]{4,3,2,1,0:T(4,128)S(1)}, f32[1,4,1,3,128]{4,3,2,1,0:T(4,128)S(1)}, f32[1,4,1,3,128]{4,3,2,1,0:T(4,128)S(1)}, f32[1,4,1,1,128]{4,3,2,1,0:T(1,128)S(1)}) custom-call(f32[2,5,2,4,128]{4,3,2,1,0:T(4,128)S(1)} %bitcast.69, f32[1,4,1,3,128]{4,3,2,1,0:T(4,128)S(1)} %get-tuple-element.58.gpos, ...), custom_call_target="tpu_custom_call" | custom-call | tf_op jit(solution)/shard_map/pallas_call | solution.py:255
  165.7 7.8 %shard_map.174 = f32[20,4,128]{2,1,0:T(4,128)S(1)} custom-call(s32[464]{0:T(512)S(1)} %get-tuple-element.42.refs_0_, s32[2,57]{1,0:T(2,128)S(1)} %get-tuple-element.43.refs_1_, f32[4,57]{1,0:T(4,128)S(1)} %get-tuple-element.44.refs_2_, s32[1]{0:T(128)} %get-tuple-element.45.refs_3_, f32[20,3,128]{2,1,0:T(4,128)S(1)} %bitcast.57, f32[20,4,128]{2,1,0:T(4,128)S(1)} %bitcast.46, ...), custom_call_target="tpu_custom_call" | custom-call | tf_op jit(solution)/shard_map/pallas_call | solution.py:450
  173.5 16.1 %shard_map.175 = (f32[2,5,2,3,128]{4,3,2,1,0:T(4,128)S(1)}, f32[1,4,1,3,128]{4,3,2,1,0:T(4,128)S(1)}, f32[1,4,1,3,128]{4,3,2,1,0:T(4,128)S(1)}, f32[1,4,1,1,128]{4,3,2,1,0:T(1,128)S(1)}) custom-call(f32[2,5,2,4,128]{4,3,2,1,0:T(4,128)S(1)} %bitcast.70, f32[1,4,1,3,128]{4,3,2,1,0:T(4,128)S(1)} %get-tuple-element.62.gpos, ...), custom_call_target="tpu_custom_call" | custom-call | tf_op jit(solution)/shard_map/pallas_call | solution.py:255
  189.6 7.8 %shard_map.176 = f32[20,4,128]{2,1,0:T(4,128)S(1)} custom-call(s32[464]{0:T(512)S(1)} %get-tuple-element.42.refs_0_, s32[2,57]{1,0:T(2,128)S(1)} %get-tuple-element.43.refs_1_, f32[4,57]{1,0:T(4,128)S(1)} %get-tuple-element.44.refs_2_, s32[1]{0:T(128)} %get-tuple-element.45.refs_3_, f32[20,3,128]{2,1,0:T(4,128)S(1)} %bitcast.55, f32[20,4,128]{2,1,0:T(4,128)S(1)} %bitcast.47, ...), custom_call_target="tpu_custom_call" | custom-call | tf_op jit(solution)/shard_map/pallas_call | solution.py:450
  197.4 16.1 %shard_map.177 = (f32[2,5,2,3,128]{4,3,2,1,0:T(4,128)S(1)}, f32[1,4,1,3,128]{4,3,2,1,0:T(4,128)S(1)}, f32[1,4,1,3,128]{4,3,2,1,0:T(4,128)S(1)}, f32[1,4,1,1,128]{4,3,2,1,0:T(1,128)S(1)}) custom-call(f32[2,5,2,4,128]{4,3,2,1,0:T(4,128)S(1)} %bitcast.67, f32[1,4,1,3,128]{4,3,2,1,0:T(4,128)S(1)} %get-tuple-element.66.gpos, ...), custom_call_target="tpu_custom_call" | custom-call | tf_op jit(solution)/shard_map/pallas_call | solution.py:255
  213.5 8.0 %shard_map.178 = f32[20,4,128]{2,1,0:T(4,128)S(1)} custom-call(s32[464]{0:T(512)S(1)} %get-tuple-element.42.refs_0_, s32[2,57]{1,0:T(2,128)S(1)} %get-tuple-element.43.refs_1_, f32[4,57]{1,0:T(4,128)S(1)} %get-tuple-element.44.refs_2_, s32[1]{0:T(128)} %get-tuple-element.45.refs_3_, f32[20,3,128]{2,1,0:T(4,128)S(1)} %bitcast.53, f32[20,4,128]{2,1,0:T(4,128)S(1)} %bitcast.48, ...), custom_call_target="tpu_custom_call" | custom-call | tf_op jit(solution)/shard_map/pallas_call | solution.py:450
  221.6 16.1 %shard_map.179 = (f32[2,5,2,3,128]{4,3,2,1,0:T(4,128)S(1)}, f32[1,4,1,3,128]{4,3,2,1,0:T(4,128)S(1)}, f32[1,4,1,3,128]{4,3,2,1,0:T(4,128)S(1)}, f32[1,4,1,1,128]{4,3,2,1,0:T(1,128)S(1)}) custom-call(f32[2,5,2,4,128]{4,3,2,1,0:T(4,128)S(1)} %bitcast.68, f32[1,4,1,3,128]{4,3,2,1,0:T(4,128)S(1)} %get-tuple-element.70.gpos, ...), custom_call_target="tpu_custom_call" | custom-call | tf_op jit(solution)/shard_map/pallas_call | solution.py:255
  237.7 7.8 %shard_map.180 = f32[20,4,128]{2,1,0:T(4,128)S(1)} custom-call(s32[464]{0:T(512)S(1)} %get-tuple-element.42.refs_0_, s32[2,57]{1,0:T(2,128)S(1)} %get-tuple-element.43.refs_1_, f32[4,57]{1,0:T(4,128)S(1)} %get-tuple-element.44.refs_2_, s32[1]{0:T(128)} %get-tuple-element.45.refs_3_, f32[20,3,128]{2,1,0:T(4,128)S(1)} %bitcast.51, f32[20,4,128]{2,1,0:T(4,128)S(1)} %bitcast.49, ...), custom_call_target="tpu_custom_call" | custom-call | tf_op jit(solution)/shard_map/pallas_call | solution.py:450
  245.5 12.8 %shard_map.181 = (f32[1,4,1,3,128]{4,3,2,1,0:T(4,128)S(1)}, f32[1,4,1,1,128]{4,3,2,1,0:T(1,128)S(1)}) custom-call(f32[2,5,2,4,128]{4,3,2,1,0:T(4,128)S(1)} %bitcast.71, f32[1,4,1,3,128]{4,3,2,1,0:T(4,128)S(1)} %get-tuple-element.74.gpos, f32[1,4,1,1,128]{4,3,2,1,0:T(1,128)S(1)} %get-tuple-element.75.charge, f32[1,4,1,1,128]{4,3,2,1,0:T(1,128)S(1)} %compare_convert_fusion.alive), custom_call_target="tpu_custom_call" | custom-call | tf_op jit(solution)/shard_map/pallas_call | solution.py:255
  (45 shorter events, 7.7 us)
Async XLA Ops:
  2.0 0.7 copy-start.7
  2.0 0.7 copy-start.4
  2.7 0.7 copy-start.5
  2.7 0.7 copy-start.8
  2.7 0.7 copy-start.9
  3.6 0.7 copy-start.6
  4.3 0.7 copy-start.3
  11.6 0.7 copy-start
  14.5 6.2 %copy-start.1 = (f32[1,4,1,3,128]{4,2,3,1,0:T(1,128)S(1)}, f32[1,4,1,3,128]{4,2,3,1,0:T(1,128)}, u32[]{:S(2)}) copy-start(f32[1,4,1,3,128]{4,2,3,1,0:T(1,128)} %param.13) | copy-start | bytes 18436
  114.8 9.5 %copy-start.2 = (f32[1,4,1,3,128]{4,2,3,1,0:T(1,128)S(1)}, f32[1,4,1,3,128]{4,2,3,1,0:T(1,128)}, u32[]{:S(2)}) copy-start(f32[1,4,1,3,128]{4,2,3,1,0:T(1,128)} %param.22) | copy-start | bytes 18436
